TPU v7x, 1024 devices: a whole 4x8x16 slice. The times are simulated.
1024 devices in a mesh: sub: 8 (over z_lo, core), lat: 128 (over x, z_hi, y).
Axes of the slice: x: 4, y: 8, z: 16 (z_hi: 4, z_lo: 4; z = z_hi * 4 + z_lo), core: 2. Of those that a mesh axis runs over, the one named last changes fastest.
Arguments:
- sources: float32 [8, 24, 524288], P(None, None, ('sub', 'lat')), may hold values from -6 to 6
- guess: float32 [8, 24, 524288], P(None, None, ('sub', 'lat')), may hold values from -6 to 6
- links: float32 [4, 18, 524288], P(None, None, ('sub', 'lat')), may hold values from -1 to 1, as said below
Outputs:
- solution: float32 [8, 24, 524288], P(None, None, ('sub', 'lat'))
Inputs may be any that keep to these rules, and one draw needn't show every extreme that they name: `links`: for each direction and site the 18 numbers are a 3 x 3 complex matrix (row, column, real and imaginary part) that is special unitary.
All inputs are finite; a program needn't handle non-finite values.
Results may differ from a plain program's by a relative error of at most 0.00002.
Values sent between devices are 32-bit elements; how exact they have to be, the bound alone decides.
A program may use at most 128 MiB of HBM per device.

v0:
```python
import functools

import jax
import jax.numpy as jnp
from jax import lax
from jax.experimental import pallas as pl
from jax.experimental.pallas import tpu as pltpu
from jax.sharding import PartitionSpec as P

HOPPING = 0.125
MESH = pl.DeviceIdType.MESH
F32 = jnp.float32
ROW = 32
LANES = 128

UPPER = (
    ((0, 0), (1, 0)),
    ((0, 1), (1, 3)),
    ((1, 2), (0, 0)),
    ((1, 1), (0, 1)),
)
LOWER = (
    ((0, 0), (1, 0)),
    ((0, 3), (1, 1)),
    ((1, 0), (0, 2)),
    ((1, 3), (0, 3)),
)


def turned(pair, power):
    re, im = pair
    return (
        ((1, re), (1, im)),
        ((-1, im), (1, re)),
        ((-1, re), (-1, im)),
        ((1, im), (-1, re)),
    )[power]


def plus(value, sign, other):
    return value + other if sign > 0 else value - other


def project(f, m, parity):
    result = []
    for spin in range(2):
        half, power = UPPER[m][spin]
        for color in range(3):
            base = (spin * 3 + color) * 2
            low = ((2 + half) * 3 + color) * 2
            parts = turned((f[low], f[low + 1]), power)
            for part in range(2):
                sign, value = parts[part]
                result.append(plus(f[base + part], -parity * sign, value))
    return result


def add_rebuilt(total, h, m, parity):
    result = []
    for index in range(12):
        result.append(h[index] if total is None else total[index] + h[index])
    for spin in range(2):
        half, power = LOWER[m][spin]
        for color in range(3):
            low = (half * 3 + color) * 2
            parts = turned((h[low], h[low + 1]), power)
            for part in range(2):
                sign, value = parts[part]
                sign = -parity * sign
                place = ((2 + spin) * 3 + color) * 2 + part
                if total is None:
                    result.append(value if sign > 0 else -value)
                else:
                    result.append(plus(total[place], sign, value))
    return result


def color_product(u, h, adjoint):
    result = []
    for spin in range(2):
        for target in range(3):
            re = im = None
            for source in range(3):
                entry = (source * 3 + target if adjoint else target * 3 + source) * 2
                ur, ui = u[entry], u[entry + 1]
                vr, vi = h[(spin * 3 + source) * 2], h[(spin * 3 + source) * 2 + 1]
                if re is None:
                    re, im = ur * vr, ur * vi
                else:
                    re, im = re + ur * vr, im + ur * vi
                if adjoint:
                    re, im = re + ui * vi, im - ui * vr
                else:
                    re, im = re - ui * vi, im + ui * vr
            result.append(re)
            result.append(im)
    return result


def roll(value, shift):
    shift = shift % LANES
    return value if shift == 0 else pltpu.roll(value, shift, 1)


def kernel(
    y_blocks, g_hbm, s_hbm, l_hbm, o_hbm, g_v, s_v, l_v, o_v, lb, x1, acc, zf, zb, zr, tf, tb, tr, yf, yb, ys, yr,
    in_sem, out_sem, zs_sem, zr_sem, ts_sem, tr_sem, ys_sem, yr_sem,
):
    sub, lat = lax.axis_index("sub"), lax.axis_index("lat")
    n_sub, n_lat = lax.axis_size("sub"), lax.axis_size("lat")
    row, column = lat // y_blocks, lat % y_blocks
    t_up, t_down = ((sub + 1) % n_sub, lat), ((sub + n_sub - 1) % n_sub, lat)
    z_up, z_down = (sub, (lat + y_blocks) % n_lat), (sub, (lat + n_lat - y_blocks) % n_lat)
    y_up = (sub, row * y_blocks + (column + 1) % y_blocks)
    y_down = (sub, row * y_blocks + (column + y_blocks - 1) % y_blocks)

    barrier = pltpu.get_barrier_semaphore()
    for other in (z_up, z_down, t_up, t_down, y_up, y_down):
        pl.semaphore_signal(barrier, inc=1, device_id=other, device_id_type=MESH)

    def lanes(cell):
        return pl.ds(cell * LANES, LANES)

    loads = [pltpu.make_async_copy(l_hbm, l_v, in_sem.at[8])]
    for cell in range(4):
        loads.append(pltpu.make_async_copy(g_hbm.at[:, lanes(cell)], g_v.at[cell], in_sem.at[cell]))
    for cell in range(4):
        loads.append(pltpu.make_async_copy(s_hbm.at[:, lanes(cell)], s_v.at[cell], in_sem.at[4 + cell]))
    for load in loads:
        load.start()

    place = lax.broadcasted_iota(jnp.int32, (16, LANES), 1)
    x_last, x_first = place % ROW == ROW - 1, place % ROW == 0
    group = place // ROW

    def spread(ref, t, comp):
        rows = pl.ds(comp, 8, stride=24)
        return jnp.concatenate([ref[2 * t, rows, :], ref[2 * t + 1, rows, :]], axis=0)

    def guess_of(t):
        return [spread(g_v, t, comp) for comp in range(24)]

    def first_of(t):
        return [x1[t, comp] for comp in range(24)]

    def link(t, m):
        return [lb[t, m, entry] for entry in range(18)]

    def copy(src, dst, send, recv, other):
        return pltpu.make_async_remote_copy(
            src_ref=src, dst_ref=dst, send_sem=send, recv_sem=recv, device_id=other, device_id_type=MESH
        )

    def z_copies(k, t):
        return [
            copy(zf.at[k, t, 0], zr.at[k, t, 0], zs_sem.at[k, t, 0], zr_sem.at[k, t, 0], z_down),
            copy(zb.at[k, t, 1], zr.at[k, t, 1], zs_sem.at[k, t, 1], zr_sem.at[k, t, 1], z_up),
        ]

    def t_copy(k, t):
        src, other = (tf, t_down) if t == 0 else (tb, t_up)
        return copy(src.at[k, t], tr.at[k, t], ts_sem.at[k, t], tr_sem.at[k, t], other)

    def y_copies(k, t):
        return [
            copy(ys.at[k, t, 0], yr.at[k, t, 0], ys_sem.at[k, t, 0], yr_sem.at[k, t, 0], y_down),
            copy(ys.at[k, t, 1], yr.at[k, t, 1], ys_sem.at[k, t, 1], yr_sem.at[k, t, 1], y_up),
        ]

    def prepare_z(k, t, field):
        f = field(t)
        ahead = project(f, 1, 1)
        behind = color_product(link(t, 1), project(f, 1, -1), True)
        for comp in range(12):
            for z in range(2):
                zf[k, t, z, comp] = ahead[comp][8 * z : 8 * z + 8]
                zb[k, t, z, comp] = behind[comp][8 * z : 8 * z + 8]

    def prepare_t(k, t, field):
        f = field(t)
        ahead = project(f, 0, 1)
        behind = color_product(link(t, 0), project(f, 0, -1), True)
        if t == 0:
            sign = jnp.where(sub == 0, -1.0, 1.0).astype(F32)
            ahead = [value * sign for value in ahead]
        else:
            sign = jnp.where(sub == n_sub - 1, -1.0, 1.0).astype(F32)
            behind = [value * sign for value in behind]
        for comp in range(12):
            tf[k, t, comp] = ahead[comp]
            tb[k, t, comp] = behind[comp]

    def prepare_y(k, t, field):
        f = field(t)
        ahead = project(f, 2, 1)
        behind = color_product(link(t, 2), project(f, 2, -1), True)
        for quad in range(3):
            packed = [None, None]
            for j in range(4):
                comp = 4 * quad + j
                up, down = roll(ahead[comp], -ROW), roll(behind[comp], ROW)
                yf[k, t, comp] = up
                yb[k, t, comp] = down
                up = up if j == 3 else roll(ahead[comp], ROW * j)
                down = down if j == 0 else roll(behind[comp], ROW * (j + 1))
                packed[0] = up if j == 0 else jnp.where(group == j, up, packed[0])
                packed[1] = down if j == 0 else jnp.where(group == j, down, packed[1])
            ys[k, t, 0, quad] = packed[0]
            ys[k, t, 1, quad] = packed[1]

    def put(t, total):
        for comp in range(24):
            acc[t, comp] = total[comp]

    def got(t):
        return [acc[t, comp] for comp in range(24)]

    def x_terms(t, field):
        f, u = field(t), link(t, 3)
        ahead = [jnp.where(x_last, roll(h, ROW - 1), roll(h, -1)) for h in project(f, 3, 1)]
        total = add_rebuilt(None, color_product(u, ahead, False), 3, 1)
        behind = color_product(u, project(f, 3, -1), True)
        behind = [jnp.where(x_first, roll(h, 1 - ROW), roll(h, 1)) for h in behind]
        put(t, add_rebuilt(total, behind, 3, -1))

    def y_terms(k, t):
        for item in y_copies(k, t):
            item.wait_recv()
        ahead, behind = [], []
        for comp in range(12):
            quad, j = comp // 4, comp % 4
            ahead.append(jnp.where(group == 3, roll(yr[k, t, 0, quad], (3 - j) * ROW), yf[k, t, comp]))
            behind.append(jnp.where(group == 0, roll(yr[k, t, 1, quad], -j * ROW), yb[k, t, comp]))
        total = add_rebuilt(got(t), color_product(link(t, 2), ahead, False), 2, 1)
        put(t, add_rebuilt(total, behind, 2, -1))

    def t_terms(k, t):
        t_copy(k, 1 - t).wait_recv()
        if t == 0:
            ahead, behind = [tf[k, 1, c] for c in range(12)], [tr[k, 1, c] for c in range(12)]
        else:
            ahead, behind = [tr[k, 0, c] for c in range(12)], [tb[k, 0, c] for c in range(12)]
        total = add_rebuilt(got(t), color_product(link(t, 0), ahead, False), 0, 1)
        put(t, add_rebuilt(total, behind, 0, -1))

    def z_terms(k, t):
        for item in z_copies(k, t):
            item.wait_recv()
        ahead = [jnp.concatenate([zf[k, t, 1, c], zr[k, t, 0, c]], axis=0) for c in range(12)]
        behind = [jnp.concatenate([zr[k, t, 1, c], zb[k, t, 0, c]], axis=0) for c in range(12)]
        total = add_rebuilt(got(t), color_product(link(t, 1), ahead, False), 1, 1)
        total = add_rebuilt(total, behind, 1, -1)
        return [spread(s_v, t, comp) + HOPPING * total[comp] for comp in range(24)]

    loads[0].wait()
    for t in range(2):
        for m in range(4):
            for entry in range(18):
                for z in range(2):
                    line = l_v[entry, m : m + 1, (2 * t + z) * LANES : (2 * t + z + 1) * LANES]
                    lb[t, m, entry, 8 * z : 8 * z + 8] = jnp.broadcast_to(line, (8, LANES))
    for load in loads[1:5]:
        load.wait()
    for t in range(2):
        prepare_z(0, t, guess_of)
        prepare_t(0, t, guess_of)
        prepare_y(0, t, guess_of)
    pl.semaphore_wait(barrier, 6)
    for item in z_copies(0, 0) + [t_copy(0, 1)] + y_copies(0, 0):
        item.start()
    for item in z_copies(0, 1) + [t_copy(0, 0)] + y_copies(0, 1):
        item.start()
    for t in range(2):
        x_terms(t, guess_of)
    for load in loads[5:]:
        load.wait()

    for t in range(2):
        y_terms(0, t)
        t_terms(0, t)
        done = z_terms(0, t)
        for comp in range(24):
            x1[t, comp] = done[comp]
        prepare_z(1, t, first_of)
        for item in z_copies(1, t):
            item.start()
        prepare_t(1, t, first_of)
        t_copy(1, t).start()
        prepare_y(1, t, first_of)
        for item in y_copies(1, t):
            item.start()
        x_terms(t, first_of)

    for t in range(2):
        y_terms(1, t)
    stores = []
    for t in range(2):
        t_terms(1, t)
        done = z_terms(1, t)
        for z in range(2):
            cell = 2 * t + z
            for comp in range(24):
                o_v[cell, pl.ds(comp, 8, stride=24), :] = done[comp][8 * z : 8 * z + 8]
            store = pltpu.make_async_copy(o_v.at[cell], o_hbm.at[:, lanes(cell)], out_sem.at[cell])
            store.start()
            stores.append(store)
    for k in range(2):
        for t in range(2):
            for item in z_copies(k, t) + [t_copy(k, t)] + y_copies(k, t):
                item.wait_send()
    for store in stores:
        store.wait()


def solution(mesh):
    y_blocks = min(8, mesh.shape["lat"] // 2)

    def on_device(sources, guess, links):
        count, parts, sites = sources.shape
        vmem, dma = pltpu.VMEM, pltpu.SemaphoreType.DMA
        anywhere = pl.BlockSpec(memory_space=pl.ANY)
        out = pl.pallas_call(
            functools.partial(kernel, y_blocks),
            out_shape=jax.ShapeDtypeStruct((count * parts, sites), F32),
            in_specs=[anywhere] * 3,
            out_specs=anywhere,
            scratch_shapes=[
                vmem((4, count * parts, LANES), F32),
                vmem((4, count * parts, LANES), F32),
                vmem((18, 4, sites), F32),
                vmem((4, count * parts, LANES), F32),
                vmem((2, 4, 18, 16, LANES), F32),
                vmem((2, 24, 16, LANES), F32),
                vmem((2, 24, 16, LANES), F32),
                vmem((2, 2, 2, 12, 8, LANES), F32),
                vmem((2, 2, 2, 12, 8, LANES), F32),
                vmem((2, 2, 2, 12, 8, LANES), F32),
                vmem((2, 2, 12, 16, LANES), F32),
                vmem((2, 2, 12, 16, LANES), F32),
                vmem((2, 2, 12, 16, LANES), F32),
                vmem((2, 2, 12, 16, LANES), F32),
                vmem((2, 2, 12, 16, LANES), F32),
                vmem((2, 2, 2, 3, 16, LANES), F32),
                vmem((2, 2, 2, 3, 16, LANES), F32),
                dma((9,)),
                dma((4,)),
                dma((2, 2, 2)),
                dma((2, 2, 2)),
                dma((2, 2)),
                dma((2, 2)),
                dma((2, 2, 2)),
                dma((2, 2, 2)),
            ],
            compiler_params=pltpu.CompilerParams(collective_id=0, has_side_effects=True),
        )(guess.reshape(count * parts, sites), sources.reshape(count * parts, sites), jnp.transpose(links, (1, 0, 2)))
        return out.reshape(sources.shape)

    spec = P(None, None, ("sub", "lat"))
    return jax.shard_map(on_device, mesh=mesh, in_specs=(spec, spec, spec), out_specs=spec, check_vma=False)
```

profile of v0, /device:TPU:24, one launch (start us, length us, event | category | flops | bytes accessed | tf_op | source)
XLA Modules:
  0.0 48.5 jit_solution(8398168082451590565)
XLA Ops:
  0.0 46.8 %shard_map.37 = f32[192,512]{1,0:T(8,128)} custom-call(f32[192,512]{1,0:T(8,128)} %bitcast.5, f32[192,512]{1,0:T(8,128)} %bitcast.6, f32[18,4,512]{2,1,0:T(4,128)} %bitcast.7), custom_call_target="tpu_custom_call" | custom-call | tf_op jit(solution)/shard_map/pallas_call | solution.py:322
  46.8 1.8 %copy.5 = f32[8,24,512]{2,1,0:T(8,128)} copy(f32[8,24,512]{2,1,0:T(8,128)} %bitcast.4) | data formatting | bytes 786432
where the time goes:
time: 48.7 us; the launch traced here: 48.5 us
  Pallas kernels  46.8 us (96%)
  local copies, waits for them, and re-layouts  1.77 us (4%)
    pallas_call x1, Pallas kernels, on_device(): pl.pallas_call(functools.partial(kernel, y_blocks), out_shape=jax.ShapeDt...  46.8 us
    unnamed x1, local copies, waits for them, and re-layouts  1.77 us

commit v1 on v0

--- a/solution.py
+++ b/solution.py
@@ -103,8 +103,8 @@
 
 
 def kernel(
-    y_blocks, g_hbm, s_hbm, l_hbm, o_hbm, g_v, s_v, l_v, o_v, lb, x1, acc, zf, zb, zr, tf, tb, tr, yf, yb, ys, yr,
-    in_sem, out_sem, zs_sem, zr_sem, ts_sem, tr_sem, ys_sem, yr_sem,
+    y_blocks, g_hbm, s_hbm, l_hbm, o_ref, g_v, s_v, l_v, lb, x1, acc, zf, zb, zr, tf, tb, tr, yf, yb, ys, yr,
+    in_sem, zs_sem, zr_sem, ts_sem, tr_sem, ys_sem, yr_sem,
 ):
     sub, lat = lax.axis_index("sub"), lax.axis_index("lat")
     n_sub, n_lat = lax.axis_size("sub"), lax.axis_size("lat")
@@ -140,9 +140,6 @@
     def guess_of(t):
         return [spread(g_v, t, comp) for comp in range(24)]
 
-    def first_of(t):
-        return [x1[t, comp] for comp in range(24)]
-
     def link(t, m):
         return [lb[t, m, entry] for entry in range(18)]
 
@@ -167,17 +164,20 @@
             copy(ys.at[k, t, 1], yr.at[k, t, 1], ys_sem.at[k, t, 1], yr_sem.at[k, t, 1], y_up),
         ]
 
-    def prepare_z(k, t, field):
-        f = field(t)
-        ahead = project(f, 1, 1)
-        behind = color_product(link(t, 1), project(f, 1, -1), True)
+    def z_rows(values, z):
+        return [value[8 * z : 8 * z + 8] for value in values]
+
+    def z_link(t, z):
+        return [lb[t, 1, entry, 8 * z : 8 * z + 8] for entry in range(18)]
+
+    def prepare_z(k, t, f, ahead_of, behind_of):
+        ahead = project(z_rows(f, ahead_of), 1, 1)
+        behind = color_product(z_link(t, behind_of), project(z_rows(f, behind_of), 1, -1), True)
         for comp in range(12):
-            for z in range(2):
-                zf[k, t, z, comp] = ahead[comp][8 * z : 8 * z + 8]
-                zb[k, t, z, comp] = behind[comp][8 * z : 8 * z + 8]
-
-    def prepare_t(k, t, field):
-        f = field(t)
+            zf[k, t, ahead_of, comp] = ahead[comp]
+            zb[k, t, behind_of, comp] = behind[comp]
+
+    def prepare_t(k, t, f):
         ahead = project(f, 0, 1)
         behind = color_product(link(t, 0), project(f, 0, -1), True)
         if t == 0:
@@ -190,8 +190,7 @@
             tf[k, t, comp] = ahead[comp]
             tb[k, t, comp] = behind[comp]
 
-    def prepare_y(k, t, field):
-        f = field(t)
+    def prepare_y(k, t, f):
         ahead = project(f, 2, 1)
         behind = color_product(link(t, 2), project(f, 2, -1), True)
         for quad in range(3):
@@ -215,13 +214,17 @@
     def got(t):
         return [acc[t, comp] for comp in range(24)]
 
-    def x_terms(t, field):
-        f, u = field(t), link(t, 3)
+    def near_terms(k, t, f):
+        u = link(t, 3)
         ahead = [jnp.where(x_last, roll(h, ROW - 1), roll(h, -1)) for h in project(f, 3, 1)]
         total = add_rebuilt(None, color_product(u, ahead, False), 3, 1)
         behind = color_product(u, project(f, 3, -1), True)
         behind = [jnp.where(x_first, roll(h, 1 - ROW), roll(h, 1)) for h in behind]
-        put(t, add_rebuilt(total, behind, 3, -1))
+        total = add_rebuilt(total, behind, 3, -1)
+        ahead = color_product(z_link(t, 0), [zf[k, t, 1, comp] for comp in range(12)], False)
+        lower = add_rebuilt(z_rows(total, 0), ahead, 1, 1)
+        upper = add_rebuilt(z_rows(total, 1), [zb[k, t, 0, comp] for comp in range(12)], 1, -1)
+        put(t, [jnp.concatenate(pair, axis=0) for pair in zip(lower, upper)])
 
     def y_terms(k, t):
         for item in y_copies(k, t):
@@ -241,75 +244,84 @@
         else:
             ahead, behind = [tr[k, 0, c] for c in range(12)], [tb[k, 0, c] for c in range(12)]
         total = add_rebuilt(got(t), color_product(link(t, 0), ahead, False), 0, 1)
-        put(t, add_rebuilt(total, behind, 0, -1))
-
-    def z_terms(k, t):
+        return add_rebuilt(total, behind, 0, -1)
+
+    def far_terms(k, t):
         for item in z_copies(k, t):
             item.wait_recv()
-        ahead = [jnp.concatenate([zf[k, t, 1, c], zr[k, t, 0, c]], axis=0) for c in range(12)]
-        behind = [jnp.concatenate([zr[k, t, 1, c], zb[k, t, 0, c]], axis=0) for c in range(12)]
-        total = add_rebuilt(got(t), color_product(link(t, 1), ahead, False), 1, 1)
-        total = add_rebuilt(total, behind, 1, -1)
-        return [spread(s_v, t, comp) + HOPPING * total[comp] for comp in range(24)]
-
-    loads[0].wait()
-    for t in range(2):
-        for m in range(4):
+        upper = color_product(z_link(t, 1), [zr[k, t, 0, comp] for comp in range(12)], False)
+        lower = add_rebuilt(None, [zr[k, t, 1, comp] for comp in range(12)], 1, -1)
+        upper = add_rebuilt(None, upper, 1, 1)
+        return [jnp.concatenate(pair, axis=0) for pair in zip(lower, upper)]
+
+    def start(*items):
+        for item in items:
+            item.start()
+
+    def spread_links(m):
+        for t in range(2):
             for entry in range(18):
                 for z in range(2):
                     line = l_v[entry, m : m + 1, (2 * t + z) * LANES : (2 * t + z + 1) * LANES]
                     lb[t, m, entry, 8 * z : 8 * z + 8] = jnp.broadcast_to(line, (8, LANES))
+
+    loads[0].wait()
+    spread_links(1)
     for load in loads[1:5]:
         load.wait()
-    for t in range(2):
-        prepare_z(0, t, guess_of)
-        prepare_t(0, t, guess_of)
-        prepare_y(0, t, guess_of)
+    prepare_z(0, 0, guess_of(0), 0, 1)
+    prepare_z(0, 1, guess_of(1), 0, 1)
     pl.semaphore_wait(barrier, 6)
-    for item in z_copies(0, 0) + [t_copy(0, 1)] + y_copies(0, 0):
-        item.start()
-    for item in z_copies(0, 1) + [t_copy(0, 0)] + y_copies(0, 1):
-        item.start()
-    for t in range(2):
-        x_terms(t, guess_of)
+    start(*z_copies(0, 0))
+    spread_links(0)
+    prepare_t(0, 1, guess_of(1))
+    prepare_t(0, 0, guess_of(0))
+    start(t_copy(0, 1), t_copy(0, 0), *z_copies(0, 1))
+    spread_links(2)
+    for t in range(2):
+        prepare_y(0, t, guess_of(t))
+        start(*y_copies(0, t))
+    spread_links(3)
+    for t in range(2):
+        prepare_z(0, t, guess_of(t), 1, 0)
+        near_terms(0, t, guess_of(t))
     for load in loads[5:]:
         load.wait()
 
     for t in range(2):
         y_terms(0, t)
-        t_terms(0, t)
-        done = z_terms(0, t)
+        total = t_terms(0, t)
+        partial = [spread(s_v, t, comp) + HOPPING * total[comp] for comp in range(24)]
+        prepare_z(1, t, partial, 0, 1)
+        start(*z_copies(1, t))
         for comp in range(24):
-            x1[t, comp] = done[comp]
-        prepare_z(1, t, first_of)
-        for item in z_copies(1, t):
-            item.start()
-        prepare_t(1, t, first_of)
-        t_copy(1, t).start()
-        prepare_y(1, t, first_of)
-        for item in y_copies(1, t):
-            item.start()
-        x_terms(t, first_of)
+            x1[t, comp] = partial[comp]
+    for t in range(2):
+        far = far_terms(0, t)
+        full = [x1[t, comp] + HOPPING * far[comp] for comp in range(24)]
+        prepare_t(1, t, full)
+        start(t_copy(1, t))
+        prepare_y(1, t, full)
+        start(*y_copies(1, t))
+        prepare_z(1, t, full, 1, 0)
+        near_terms(1, t, full)
 
     for t in range(2):
         y_terms(1, t)
-    stores = []
-    for t in range(2):
-        t_terms(1, t)
-        done = z_terms(1, t)
+    for t in range(2):
+        total = t_terms(1, t)
+        put(t, [spread(s_v, t, comp) + HOPPING * total[comp] for comp in range(24)])
+    for t in range(2):
+        far = far_terms(1, t)
+        done = [acc[t, comp] + HOPPING * far[comp] for comp in range(24)]
         for z in range(2):
             cell = 2 * t + z
             for comp in range(24):
-                o_v[cell, pl.ds(comp, 8, stride=24), :] = done[comp][8 * z : 8 * z + 8]
-            store = pltpu.make_async_copy(o_v.at[cell], o_hbm.at[:, lanes(cell)], out_sem.at[cell])
-            store.start()
-            stores.append(store)
+                o_ref[pl.ds(comp // 8 * 32 + cell * 8 + comp % 8, 8, stride=96), :] = done[comp][8 * z : 8 * z + 8]
     for k in range(2):
         for t in range(2):
             for item in z_copies(k, t) + [t_copy(k, t)] + y_copies(k, t):
                 item.wait_send()
-    for store in stores:
-        store.wait()
 
 
 def solution(mesh):
@@ -318,17 +330,16 @@
     def on_device(sources, guess, links):
         count, parts, sites = sources.shape
         vmem, dma = pltpu.VMEM, pltpu.SemaphoreType.DMA
-        anywhere = pl.BlockSpec(memory_space=pl.ANY)
+        anywhere = pl.BlockSpec(memory_space=pltpu.HBM)
         out = pl.pallas_call(
             functools.partial(kernel, y_blocks),
-            out_shape=jax.ShapeDtypeStruct((count * parts, sites), F32),
+            out_shape=jax.ShapeDtypeStruct((count * parts * sites // LANES, LANES), F32),
             in_specs=[anywhere] * 3,
-            out_specs=anywhere,
+            out_specs=pl.BlockSpec(memory_space=pltpu.VMEM),
             scratch_shapes=[
                 vmem((4, count * parts, LANES), F32),
                 vmem((4, count * parts, LANES), F32),
                 vmem((18, 4, sites), F32),
-                vmem((4, count * parts, LANES), F32),
                 vmem((2, 4, 18, 16, LANES), F32),
                 vmem((2, 24, 16, LANES), F32),
                 vmem((2, 24, 16, LANES), F32),
@@ -343,7 +354,6 @@
                 vmem((2, 2, 2, 3, 16, LANES), F32),
                 vmem((2, 2, 2, 3, 16, LANES), F32),
                 dma((9,)),
-                dma((4,)),
                 dma((2, 2, 2)),
                 dma((2, 2, 2)),
                 dma((2, 2)),
@@ -351,9 +361,9 @@
                 dma((2, 2, 2)),
                 dma((2, 2, 2)),
             ],
-            compiler_params=pltpu.CompilerParams(collective_id=0, has_side_effects=True),
-        )(guess.reshape(count * parts, sites), sources.reshape(count * parts, sites), jnp.transpose(links, (1, 0, 2)))
-        return out.reshape(sources.shape)
+            compiler_params=pltpu.CompilerParams(collective_id=0, has_side_effects=True, vmem_limit_bytes=16 << 20),
+        )(*[pltpu.with_memory_space_constraint(a, pltpu.HBM) for a in (guess.reshape(count * parts, sites), sources.reshape(count * parts, sites), jnp.transpose(links, (1, 0, 2)))])
+        return jnp.transpose(out.reshape(count * parts // 8, sites // LANES, 8, LANES), (0, 2, 1, 3)).reshape(sources.shape)
 
     spec = P(None, None, ("sub", "lat"))
     return jax.shard_map(on_device, mesh=mesh, in_specs=(spec, spec, spec), out_specs=spec, check_vma=False)

time: 48.7 us -> 44.1 us (0.906)
  the two profiles are of different devices: /device:TPU:24 before, /device:TPU:1 now
where the time goes in v1:
time: 44.1 us; the launch traced here: 43.9 us
  Pallas kernels  43.2 us (98%)
  local copies, waits for them, and re-layouts  0.75 us (2%)
    pallas_call x1, Pallas kernels, on_device(): pl.pallas_call(functools.partial(kernel, y_blocks), out_shape=jax.ShapeDt...  43.2 us

profile of v1, /device:TPU:1, one launch (start us, length us, event | category | flops | bytes accessed | tf_op | source)
XLA Modules:
  0.0 43.9 jit_solution(2436950028440066213)
XLA Ops:
  0.0 43.2 %shard_map.37 = f32[768,128]{1,0:T(8,128)S(1)} custom-call(f32[192,512]{1,0:T(8,128)} %bitcast.9, f32[192,512]{1,0:T(8,128)} %bitcast.10, f32[18,4,512]{2,1,0:T(4,128)} %bitcast.11), custom_call_target="tpu_custom_call" | custom-call | tf_op jit(solution)/shard_map/pallas_call | solution.py:334
  43.2 0.7 %copy.5 = f32[8,24,512]{2,1,0:T(8,128)} copy(f32[8,24,512]{2,1,0:T(8,128)S(1)} %bitcast.8) | data formatting | bytes 786432
